TPU v7x, 128 devices: a whole 4x4x4 slice. The times are simulated.
128 devices in a mesh: feat: 64 (over x, y, z_lo, core), rows: 2 (over z_hi).
Axes of the slice: x: 4, y: 4, z: 4 (z_hi: 2, z_lo: 2; z = z_hi * 2 + z_lo), core: 2. Of those that a mesh axis runs over, the one named last changes fastest.
Arguments:
- embeddings: bfloat16 [256, 512], P('rows'), may hold values from -6 to 6
- sign_flips: float32 [524288], P('feat'), may hold values from -1 to 1, as said below
- gaussian: float32 [524288], P('feat'), may hold values from -5 to 5
- scales: float32 [524288], P('feat'), may hold values from 0.5 to 2
- phases: float32 [524288], P('feat'), may hold values from 0 to 6.2831855
- source_blocks: int32 [4096], P('feat'), may hold values from 0 to 4095, as said below
- block_permutations: bfloat16 [4096, 128, 128], P('feat'), may hold values from 0 to 1, as said below
- weights: float32 [524288], P('feat'), may hold values from -6 to 6
- targets: float32 [256], P('rows'), may hold values from -6 to 6
Outputs:
- predictions: float32 [256], P('rows')
- feature_grad: float32 [524288], P(('feat', 'rows'))
Inputs may be any that keep to these rules, and one draw needn't show every extreme that they name: `sign_flips`: each entry is -1 or 1. `source_blocks`: A permutation of the 4096 block numbers. The 64 entries of each aligned run of 64 entries name exactly 1 block from every aligned run of 64 blocks. Each block_permutations[b] is a permutation matrix.
All inputs are finite; a program needn't handle non-finite values.
Results may differ from a plain program's by a relative error of at most 0.0003.
Values sent between devices are 32-bit elements; how exact they have to be, the bound alone decides.
A program may use at most 64 MiB of HBM per device.

v0:
```python
import math
import jax
import jax.numpy as jnp
from jax import lax
from jax.sharding import PartitionSpec as P

FEATURE_COUNT = 524288


def rademacher_signs(length):
    indices = jnp.arange(length, dtype=jnp.int32)
    joined = jnp.bitwise_and(indices[:, None], indices[None, :])
    parity = jnp.zeros((length, length), jnp.int32)
    for bit_number in range(length.bit_length() - 1):
        parity = parity + jnp.bitwise_and(jnp.right_shift(joined, bit_number), 1)
    return (1 - 2 * jnp.bitwise_and(parity, 1)).astype(jnp.float32)


def transform(field, block):
    row_count = field.shape[0]
    feat_here = field.shape[1]
    outer = feat_here // block
    values = field.reshape(row_count, outer, block)
    values = jnp.einsum(
        "rac,dc->rad", values, rademacher_signs(block), precision=lax.Precision.HIGHEST
    )
    values = jnp.einsum(
        "rac,ba->rbc", values, rademacher_signs(outer), precision=lax.Precision.HIGHEST
    )
    device_shards = lax.axis_size("feat")
    spread = values
    across_devices = lax.all_to_all(spread, "feat", split_axis=1, concat_axis=1, tiled=True)
    combined = jnp.einsum(
        "gwf,aw->gaf",
        across_devices,
        rademacher_signs(device_shards),
        precision=lax.Precision.HIGHEST,
    )
    returned = lax.all_to_all(combined, "feat", split_axis=1, concat_axis=1, tiled=True)
    values = returned.reshape(row_count, feat_here)
    return values * (1.0 / math.sqrt(FEATURE_COUNT))


def local(
    embeddings,
    sign_flips,
    gaussian,
    scales,
    phases,
    source_blocks,
    block_permutations,
    weights,
    targets,
):
    row_count = embeddings.shape[0]
    width = embeddings.shape[1]
    feat_here = sign_flips.shape[0]
    blk_here = block_permutations.shape[0]
    block = block_permutations.shape[1]
    device_shards = lax.axis_size("feat")
    per_pair = blk_here // device_shards
    tiled = jnp.tile(embeddings.astype(jnp.float32), (1, feat_here // width)) * sign_flips[None, :]
    first = transform(tiled, block)
    source_dev = source_blocks // blk_here
    source_local = source_blocks % blk_here
    slot_keys = source_dev * blk_here + jnp.arange(blk_here, dtype=jnp.int32)
    ordering = jnp.argsort(slot_keys)
    inverse = jnp.argsort(ordering)
    wanted = jnp.take(source_local, ordering).reshape(device_shards, per_pair)
    asked = lax.all_to_all(wanted, "feat", split_axis=0, concat_axis=0, tiled=True)
    first_blocks = first.reshape(row_count, blk_here, block)
    outgoing = jnp.take(first_blocks, asked.reshape(-1), axis=1)
    incoming = lax.all_to_all(outgoing, "feat", split_axis=1, concat_axis=1, tiled=True)
    placed = jnp.take(incoming, inverse, axis=1)
    mixed = jnp.einsum(
        "rbj,bij->rbi",
        placed,
        block_permutations.astype(jnp.float32),
        precision=lax.Precision.HIGHEST,
    )
    mixed = mixed.reshape(row_count, feat_here) * gaussian[None, :]
    second = transform(mixed, block)
    features = jnp.cos(scales[None, :] * second + phases[None, :])
    local_sum = jnp.dot(features, weights, precision=lax.Precision.HIGHEST)
    predictions = lax.psum(local_sum, "feat") * (1.0 / math.sqrt(FEATURE_COUNT))
    residual = predictions - targets
    total_rows = row_count * lax.axis_size("rows")
    grad_terms = jnp.dot(residual, features, precision=lax.Precision.HIGHEST) * (
        1.0 / math.sqrt(total_rows)
    )
    feature_grad = lax.psum_scatter(grad_terms, "rows", scatter_dimension=0, tiled=True)
    return (predictions, feature_grad)


def solution(mesh):
    in_specs = (
        P("rows", None),
        P("feat"),
        P("feat"),
        P("feat"),
        P("feat"),
        P("feat"),
        P("feat", None, None),
        P("feat"),
        P("rows"),
    )
    out_specs = (P("rows"), P(("feat", "rows")))
    return jax.shard_map(local, mesh=mesh, in_specs=in_specs, out_specs=out_specs, check_vma=False)
```

profile of v0, /device:TPU:0, one launch (start us, length us, event | category | flops | bytes accessed | tf_op | source)
XLA Modules:
  0.0 581.3 jit_solution(2201603233594802488)
XLA Ops:
  0.6 0.0 copy-start
  0.6 3.5 tile.4
  4.2 4.8 tile.10
  8.9 6.5 %fusion.11 = f32[128,64,128]{2,1,0:T(8,128)S(1)} fusion(f32[128,64,128]{2,1,0:T(8,128)} %tile.10, f32[64,128]{1,0:T(8,128)S(1)} %bitcast.56), kind=kOutput, calls=%fused_computation.17 | convolution fusion | flops 1612070912 | bytes 8421376 | tf_op jit(solution)/shard_map/rac,dc->rad/dot_general | solution.py:24
  15.5 3.9 convolution_bitcast_fusion.1
  19.3 4.4 copy.25
  23.7 9.8 %all-to-all-start = ((f32[128,64,128]{2,0,1:T(8,128)}), f32[128,64,128]{2,0,1:T(8,128)}, u32[]{:S(2)}, u32[]{:S(2)}) async-start(f32[128,64,128]{2,0,1:T(8,128)} %copy.25), calls=%async_computation | async-start | bytes 8388608 | tf_op jit(solution)/shard_map/all_to_all | solution.py:32
  33.6 2.0 sort.31
  35.6 0.8 gather_fusion
  36.4 0.7 copy.24
  37.1 47.5 %all-to-all-done = f32[128,64,128]{2,0,1:T(8,128)} async-done(((f32[128,64,128]{2,0,1:T(8,128)}), f32[128,64,128]{2,0,1:T(8,128)}, u32[]{:S(2)}, u32[]{:S(2)}) %all-to-all-start) | async-done | bytes 4194336 | tf_op jit(solution)/shard_map/all_to_all | solution.py:32
  84.6 9.3 %all-to-all-start.2 = ((s32[64,1,1]{2,1,0:T(1,128)}), s32[64,1,1]{2,1,0:T(1,128)S(1)}, u32[]{:S(2)}, u32[]{:S(2)}) async-start(s32[64,1,1]{2,1,0:T(1,128)} %copy.24), calls=%async_computation.2 | async-start | bytes 65536 | tf_op jit(solution)/shard_map/all_to_all | solution.py:70
  93.9 8.4 %fusion.13 = f32[128,64,128]{2,1,0:T(8,128)S(1)} fusion(f32[128,64,128]{2,0,1:T(8,128)} %all-to-all-done), kind=kOutput, calls=%fused_computation.19 | convolution fusion | flops 805396480 | bytes 8388608 | tf_op jit(solution)/shard_map/gwf,aw->gaf/dot_general | solution.py:33
  102.3 4.4 copy.27
  106.7 0.0 all-to-all-done.2
  106.7 9.2 %all-to-all-start.1 = ((f32[128,64,128]{2,0,1:T(8,128)}), f32[128,64,128]{2,0,1:T(8,128)}, u32[]{:S(2)}, u32[]{:S(2)}) async-start(f32[128,64,128]{2,0,1:T(8,128)} %copy.27), calls=%async_computation.1 | async-start | bytes 8388608 | tf_op jit(solution)/shard_map/all_to_all | solution.py:39
  116.0 1.2 reduce
  117.2 49.8 %all-to-all-done.1 = f32[128,64,128]{2,0,1:T(8,128)} async-done(((f32[128,64,128]{2,0,1:T(8,128)}), f32[128,64,128]{2,0,1:T(8,128)}, u32[]{:S(2)}, u32[]{:S(2)}) %all-to-all-start.1) | async-done | bytes 4194336 | tf_op jit(solution)/shard_map/all_to_all | solution.py:39
  167.1 4.9 broadcast_multiply_fusion
  172.0 4.9 gather_fusion.1
  176.9 4.5 select_bitcast_fusion
  181.3 9.4 %all-to-all-start.3 = ((f32[128,64,128]{2,0,1:T(8,128)}), f32[128,64,128]{2,0,1:T(8,128)}, u32[]{:S(2)}, u32[]{:S(2)}) async-start(f32[128,64,128]{2,0,1:T(8,128)} %select_bitcast_fusion), calls=%async_computation.3 | async-start | bytes 8388608 | tf_op jit(solution)/shard_map/all_to_all | solution.py:73
  190.7 2.0 sort.32
  192.8 0.0 copy-start.4
  192.8 49.0 %all-to-all-done.3 = f32[128,64,128]{2,0,1:T(8,128)} async-done(((f32[128,64,128]{2,0,1:T(8,128)}), f32[128,64,128]{2,0,1:T(8,128)}, u32[]{:S(2)}, u32[]{:S(2)}) %all-to-all-start.3) | async-done | bytes 4194336 | tf_op jit(solution)/shard_map/all_to_all | solution.py:73
  241.8 4.9 gather_fusion.2
  246.7 0.0 copy-done
  246.7 6.5 %multiply_bitcast_fusion = f32[128,64,128]{2,0,1:T(8,128)S(1)} fusion(bf16[64,128,128]{2,1,0:T(8,128)(2,1)S(1)} %copy-done, f32[64,128,128]{2,1,0:T(8,128)} %gather_fusion.2, f32[64,128]{1,0:T(8,128)S(1)} %bitcast.57, pred[64]{0:T(512)(128)(4,1)S(1)} %compare_and_fusion), kind=kOutput, calls=%fused_computation.16 | convolution fusion | flops 1612709888 | bytes 10518592 | tf_op jit(solution)/shard_map/rbj,bij->rbi/dot_general | solution.py:75
  253.3 6.5 %fusion.6 = f32[128,64,128]{2,1,0:T(8,128)S(1)} fusion(f32[128,64,128]{2,0,1:T(8,128)S(1)} %multiply_bitcast_fusion), kind=kOutput, calls=%fused_computation.10 | convolution fusion | flops 1611022336 | bytes 8388608 | tf_op jit(solution)/shard_map/rac,dc->rad/dot_general | solution.py:24
  259.8 3.9 convolution_bitcast_fusion
  263.7 2.8 copy.29
  266.5 60.0 %all_to_all.31 = f32[128,64,128]{2,0,1:T(8,128)S(1)} all-to-all(f32[128,64,128]{2,0,1:T(8,128)S(1)} %copy.29), channel_id=1, replica_groups=mesh['feat'=64,'rows'=2] {'feat'}, dimensions={1} | all-to-all | bytes 8388608 | tf_op jit(solution)/shard_map/all_to_all | solution.py:32
  326.5 6.0 %fusion.16 = f32[128,64,128]{2,1,0:T(8,128)S(1)} fusion(f32[128,64,128]{2,0,1:T(8,128)S(1)} %all_to_all.31), kind=kOutput, calls=%fused_computation.20 | convolution fusion | flops 805396480 | bytes 8388608 | tf_op jit(solution)/shard_map/gwf,aw->gaf/dot_general | solution.py:33
  332.5 4.4 copy.31
  336.9 6.1 %all-to-all-start.5 = ((f32[128,64,128]{2,0,1:T(8,128)}), f32[128,64,128]{2,0,1:T(8,128)}, u32[]{:S(2)}, u32[]{:S(2)}) async-start(f32[128,64,128]{2,0,1:T(8,128)} %copy.31), calls=%async_computation.5 | async-start | bytes 8388608 | tf_op jit(solution)/shard_map/all_to_all | solution.py:39
  343.0 0.6 dynamic-slice
  344.3 0.0 copy-start.5
  344.3 49.6 %all-to-all-done.5 = f32[128,64,128]{2,0,1:T(8,128)} async-done(((f32[128,64,128]{2,0,1:T(8,128)}), f32[128,64,128]{2,0,1:T(8,128)}, u32[]{:S(2)}, u32[]{:S(2)}) %all-to-all-start.5) | async-done | bytes 4194336 | tf_op jit(solution)/shard_map/all_to_all | solution.py:39
  393.9 5.6 copy.32
  399.5 16.6 %fusion.1 = f32[128,8192]{0,1:T(8,128)S(1)} fusion(f32[128,64,128]{0,2,1:T(8,128)} %copy.32, f32[8192]{0:T(1024)S(1)} %copy-done.5, f32[8192]{0:T(1024)S(1)} %broadcast_multiply_fusion.2), kind=kLoop, calls=%fused_computation.5 | loop fusion | flops 2097152 | bytes 8454144 | tf_op jit(solution)/shard_map/cos | solution.py:83
  416.1 0.0 copy-start.8
  416.1 0.0 copy-start.1
  416.2 2.1 copy-done.2
  418.3 2.3 convolution_bitcast_fusion.2
  420.6 142.3 %psum.7 = f32[128]{0:T(128)S(1)} all-reduce(f32[128]{0:T(128)S(1)} %convolution_bitcast_fusion.2), channel_id=1, replica_groups=mesh['feat'=64,'rows'=2] {'feat'}, use_global_device_ids=true, to_apply=%region_2.4 | all-reduce | flops 128 | bytes 1024 | tf_op jit(solution)/shard_map/psum | solution.py:85
  562.9 5.6 fusion.36
  568.6 11.9 %all-reduce = f32[8192]{0:T(1024)S(1)} all-reduce(f32[8192]{0:T(1024)S(1)} %broadcast_multiply_fusion.1), channel_id=2, replica_groups=mesh['feat'=64,'rows'=2] {'rows'}, use_global_device_ids=true, to_apply=%region_3.5.clone | all-reduce | flops 8192 | bytes 65536
  580.5 0.6 dynamic-slice.1
  (32 shorter events, 0.1 us)
Async XLA Ops:
  0.6 246.1 %copy-start = (bf16[64,128,128]{2,1,0:T(8,128)(2,1)S(1)}, bf16[64,128,128]{2,1,0:T(8,128)(2,1)}, u32[]{:S(2)}) copy-start(bf16[64,128,128]{2,1,0:T(8,128)(2,1)} %param.17) | copy-start | bytes 6291460
  4.2 4.8 copy-start.3
  23.7 9.8 %copy-start.10 = (s32[64]{0:T(128)S(1)}, s32[64]{0:T(128)}, u32[]{:S(2)}) copy-start(s32[64]{0:T(128)} %param.16) | copy-start | bytes 772
  23.7 60.9 %all-to-all-start = ((f32[128,64,128]{2,0,1:T(8,128)}), f32[128,64,128]{2,0,1:T(8,128)}, u32[]{:S(2)}, u32[]{:S(2)}) async-start(f32[128,64,128]{2,0,1:T(8,128)} %copy.25), calls=%async_computation | async-start | bytes 8388608 | tf_op jit(solution)/shard_map/all_to_all | solution.py:32
  84.6 22.1 %all-to-all-start.2 = ((s32[64,1,1]{2,1,0:T(1,128)}), s32[64,1,1]{2,1,0:T(1,128)S(1)}, u32[]{:S(2)}, u32[]{:S(2)}) async-start(s32[64,1,1]{2,1,0:T(1,128)} %copy.24), calls=%async_computation.2 | async-start | bytes 65536 | tf_op jit(solution)/shard_map/all_to_all | solution.py:70
  106.7 60.3 %all-to-all-start.1 = ((f32[128,64,128]{2,0,1:T(8,128)}), f32[128,64,128]{2,0,1:T(8,128)}, u32[]{:S(2)}, u32[]{:S(2)}) async-start(f32[128,64,128]{2,0,1:T(8,128)} %copy.27), calls=%async_computation.1 | async-start | bytes 8388608 | tf_op jit(solution)/shard_map/all_to_all | solution.py:39
  181.3 60.5 %all-to-all-start.3 = ((f32[128,64,128]{2,0,1:T(8,128)}), f32[128,64,128]{2,0,1:T(8,128)}, u32[]{:S(2)}, u32[]{:S(2)}) async-start(f32[128,64,128]{2,0,1:T(8,128)} %select_bitcast_fusion), calls=%async_computation.3 | async-start | bytes 8388608 | tf_op jit(solution)/shard_map/all_to_all | solution.py:73
  192.8 54.0 %copy-start.4 = (f32[8192]{0:T(1024)S(1)}, f32[8192]{0:T(1024)}, u32[]{:S(2)}) copy-start(f32[8192]{0:T(1024)} %param.13) | copy-start | bytes 98308
  336.9 6.1 %copy-start.11 = (u32[128]{0:T(128)S(1)}, u32[128]{0:T(128)}, u32[]{:S(2)}) copy-start(u32[128]{0:T(128)} %constant.76) | copy-start | bytes 1540
  336.9 7.4 %copy-start.7 = (f32[8192]{0:T(1024)S(1)}, f32[8192]{0:T(1024)}, u32[]{:S(2)}) copy-start(f32[8192]{0:T(1024)} %param.14) | copy-start | bytes 98308
  336.9 57.0 %all-to-all-start.5 = ((f32[128,64,128]{2,0,1:T(8,128)}), f32[128,64,128]{2,0,1:T(8,128)}, u32[]{:S(2)}, u32[]{:S(2)}) async-start(f32[128,64,128]{2,0,1:T(8,128)} %copy.31), calls=%async_computation.5 | async-start | bytes 8388608 | tf_op jit(solution)/shard_map/all_to_all | solution.py:39
  344.3 55.2 %copy-start.5 = (f32[8192]{0:T(1024)S(1)}, f32[8192]{0:T(1024)}, u32[]{:S(2)}) copy-start(f32[8192]{0:T(1024)} %param.15) | copy-start | bytes 98308
  399.5 18.8 %copy-start.6 = (f32[8192]{0:T(1024)S(1)}, f32[8192]{0:T(1024)}, u32[]{:S(2)}) copy-start(f32[8192]{0:T(1024)} %param.18) | copy-start | bytes 98308
  416.1 2.1 copy-start.2
  416.1 146.8 %copy-start.8 = (f32[128]{0:T(128)S(1)}, f32[128]{0:T(128)}, u32[]{:S(2)}) copy-start(f32[128]{0:T(128)} %param.19) | copy-start | bytes 1540
  416.1 165.0 %copy-start.1 = (bf16[64,128,128]{2,1,0:T(8,128)(2,1)S(1)}, bf16[64,128,128]{2,1,0:T(8,128)(2,1)}, u32[]{:S(2)}) copy-start(bf16[64,128,128]{2,1,0:T(8,128)(2,1)} %param.17) | copy-start | bytes 6291460
  562.9 18.2 %copy-start.9 = (f32[128]{0:T(128)}, f32[128]{0:T(128)S(1)}, u32[]{:S(2)}) copy-start(f32[128]{0:T(128)S(1)} %broadcast_multiply_fusion.3) | copy-start | bytes 1540
where the time goes:
time: 591 us; the launch traced here: 581 us
  blocking collectives  214 us (36%)
  waiting for transfers between devices  196 us (33%)
  matrix products  49.6 us (8%)
  local copies, waits for them, and re-layouts  44.6 us (8%)
  starting transfers between devices  43.8 us (7%)
  other arithmetic  31.4 us (5%)
    psum x1, blocking collectives, local(): predictions = lax.psum(local_sum, 'feat') * (1.0 / math.sqrt(FEATURE_COUNT))  142 us
    all_to_all x2, waiting for transfers between devices, transform(): lax.all_to_all(combined, 'feat', split_axis=1, concat_axis=1, tiled=True)  99.5 us
    all_to_all x1, blocking collectives, transform(): lax.all_to_all(spread, 'feat', split_axis=1, concat_axis=1, tiled=True)  60 us
    all_to_all x1, waiting for transfers between devices, local(): lax.all_to_all(outgoing, 'feat', split_axis=1, concat_axis=1, tiled=True)  49 us
    all_to_all x1, waiting for transfers between devices, transform(): lax.all_to_all(spread, 'feat', split_axis=1, concat_axis=1, tiled=True)  47.5 us
    cos x1, other arithmetic, local(): features = jnp.cos(scales[None, :] * second + phases[None, :])  16.6 us
    all_to_all x2, starting transfers between devices, transform(): lax.all_to_all(combined, 'feat', split_axis=1, concat_axis=1, tiled=True)  15.3 us
    dot_general x2, matrix products, transform(): jnp.einsum('gwf,aw->gaf', across_devices, rademacher_signs(device_shards)...  14.4 us
  transfers between devices with their start and end apart: 5, of which 4 were waited for; matrix products, arithmetic and copies ran while one was open for 3% of the time, Pallas kernels for 0%

commit v1 on v0

--- a/solution.py
+++ b/solution.py
@@ -82,7 +82,9 @@
     second = transform(mixed, block)
     features = jnp.cos(scales[None, :] * second + phases[None, :])
     local_sum = jnp.dot(features, weights, precision=lax.Precision.HIGHEST)
-    predictions = lax.psum(local_sum, "feat") * (1.0 / math.sqrt(FEATURE_COUNT))
+    predictions = jnp.sum(lax.all_gather(local_sum, "feat"), axis=0) * (
+        1.0 / math.sqrt(FEATURE_COUNT)
+    )
     residual = predictions - targets
     total_rows = row_count * lax.axis_size("rows")
     grad_terms = jnp.dot(residual, features, precision=lax.Precision.HIGHEST) * (

time: 591 us -> 529 us (0.90)
  blocking collectives: 214 us -> 152 us
    psum x1 -> x0, blocking collectives: 142 us -> none  [local(): predictions = lax.psum(local_sum, 'feat') * (1.0 / math.sqrt(FEATURE_COUNT))]
    all_gather x0 -> x1, blocking collectives: none -> 80.4 us  [local(): lax.all_gather(local_sum, 'feat')]
  transfers between devices with their start and end apart: 5 -> 5, of which waited for: 4 -> 4; matrix products, arithmetic and copies ran while one was open for 3% -> 4% of each run, Pallas kernels for 0% -> 0%
where the time goes in v1:
time: 529 us; the launch traced here: 520 us
  waiting for transfers between devices  196 us (37%)
  blocking collectives  152 us (29%)
  matrix products  49.6 us (9%)
  local copies, waits for them, and re-layouts  44.6 us (8%)
  starting transfers between devices  43.8 us (8%)
  other arithmetic  31.5 us (6%)
    all_to_all x2, waiting for transfers between devices, transform(): lax.all_to_all(combined, 'feat', split_axis=1, concat_axis=1, tiled=True)  99.5 us
    all_gather x1, blocking collectives, local(): lax.all_gather(local_sum, 'feat')  80.4 us
    all_to_all x1, blocking collectives, transform(): lax.all_to_all(spread, 'feat', split_axis=1, concat_axis=1, tiled=True)  60 us
    all_to_all x1, waiting for transfers between devices, local(): lax.all_to_all(outgoing, 'feat', split_axis=1, concat_axis=1, tiled=True)  49 us
    all_to_all x1, waiting for transfers between devices, transform(): lax.all_to_all(spread, 'feat', split_axis=1, concat_axis=1, tiled=True)  47.5 us
    cos x1, other arithmetic, local(): features = jnp.cos(scales[None, :] * second + phases[None, :])  16.6 us
    all_to_all x2, starting transfers between devices, transform(): lax.all_to_all(combined, 'feat', split_axis=1, concat_axis=1, tiled=True)  15.3 us
    dot_general x2, matrix products, transform(): jnp.einsum('gwf,aw->gaf', across_devices, rademacher_signs(device_shards)...  14.4 us
  transfers between devices with their start and end apart: 5, of which 4 were waited for; matrix products, arithmetic and copies ran while one was open for 4% of the time, Pallas kernels for 0%

profile of v1, /device:TPU:0, one launch (start us, length us, event | category | flops | bytes accessed | tf_op | source)
XLA Modules:
  0.0 519.5 jit_solution(9048397947707734252)
XLA Ops:
  0.6 0.0 copy-start
  0.6 3.5 tile.4
  4.2 4.8 tile.10
  8.9 6.5 %fusion.11 = f32[128,64,128]{2,1,0:T(8,128)S(1)} fusion(f32[128,64,128]{2,1,0:T(8,128)} %tile.10, f32[64,128]{1,0:T(8,128)S(1)} %bitcast.58), kind=kOutput, calls=%fused_computation.17 | convolution fusion | flops 1612070912 | bytes 8421376 | tf_op jit(solution)/shard_map/rac,dc->rad/dot_general | solution.py:24
  15.5 3.9 convolution_bitcast_fusion.1
  19.3 4.4 copy.25
  23.7 9.8 %all-to-all-start = ((f32[128,64,128]{2,0,1:T(8,128)}), f32[128,64,128]{2,0,1:T(8,128)}, u32[]{:S(2)}, u32[]{:S(2)}) async-start(f32[128,64,128]{2,0,1:T(8,128)} %copy.25), calls=%async_computation | async-start | bytes 8388608 | tf_op jit(solution)/shard_map/all_to_all | solution.py:32
  33.6 2.0 sort.31
  35.6 0.8 gather_fusion
  36.4 0.7 copy.24
  37.1 47.5 %all-to-all-done = f32[128,64,128]{2,0,1:T(8,128)} async-done(((f32[128,64,128]{2,0,1:T(8,128)}), f32[128,64,128]{2,0,1:T(8,128)}, u32[]{:S(2)}, u32[]{:S(2)}) %all-to-all-start) | async-done | bytes 4194336 | tf_op jit(solution)/shard_map/all_to_all | solution.py:32
  84.6 9.3 %all-to-all-start.2 = ((s32[64,1,1]{2,1,0:T(1,128)}), s32[64,1,1]{2,1,0:T(1,128)S(1)}, u32[]{:S(2)}, u32[]{:S(2)}) async-start(s32[64,1,1]{2,1,0:T(1,128)} %copy.24), calls=%async_computation.2 | async-start | bytes 65536 | tf_op jit(solution)/shard_map/all_to_all | solution.py:70
  93.9 8.4 %fusion.13 = f32[128,64,128]{2,1,0:T(8,128)S(1)} fusion(f32[128,64,128]{2,0,1:T(8,128)} %all-to-all-done), kind=kOutput, calls=%fused_computation.19 | convolution fusion | flops 805396480 | bytes 8388608 | tf_op jit(solution)/shard_map/gwf,aw->gaf/dot_general | solution.py:33
  102.3 4.4 copy.27
  106.7 9.2 %all-to-all-start.1 = ((f32[128,64,128]{2,0,1:T(8,128)}), f32[128,64,128]{2,0,1:T(8,128)}, u32[]{:S(2)}, u32[]{:S(2)}) async-start(f32[128,64,128]{2,0,1:T(8,128)} %copy.27), calls=%async_computation.1 | async-start | bytes 8388608 | tf_op jit(solution)/shard_map/all_to_all | solution.py:39
  116.0 1.2 reduce.1
  117.2 49.8 %all-to-all-done.1 = f32[128,64,128]{2,0,1:T(8,128)} async-done(((f32[128,64,128]{2,0,1:T(8,128)}), f32[128,64,128]{2,0,1:T(8,128)}, u32[]{:S(2)}, u32[]{:S(2)}) %all-to-all-start.1) | async-done | bytes 4194336 | tf_op jit(solution)/shard_map/all_to_all | solution.py:39
  167.1 4.9 broadcast_multiply_fusion
  172.0 4.9 gather_fusion.1
  176.9 4.5 select_bitcast_fusion
  181.3 9.4 %all-to-all-start.3 = ((f32[128,64,128]{2,0,1:T(8,128)}), f32[128,64,128]{2,0,1:T(8,128)}, u32[]{:S(2)}, u32[]{:S(2)}) async-start(f32[128,64,128]{2,0,1:T(8,128)} %select_bitcast_fusion), calls=%async_computation.3 | async-start | bytes 8388608 | tf_op jit(solution)/shard_map/all_to_all | solution.py:73
  190.7 2.0 sort.32
  192.8 0.0 copy-start.4
  192.8 49.0 %all-to-all-done.3 = f32[128,64,128]{2,0,1:T(8,128)} async-done(((f32[128,64,128]{2,0,1:T(8,128)}), f32[128,64,128]{2,0,1:T(8,128)}, u32[]{:S(2)}, u32[]{:S(2)}) %all-to-all-start.3) | async-done | bytes 4194336 | tf_op jit(solution)/shard_map/all_to_all | solution.py:73
  241.8 4.9 gather_fusion.2
  246.7 6.5 %multiply_bitcast_fusion = f32[128,64,128]{2,0,1:T(8,128)S(1)} fusion(bf16[64,128,128]{2,1,0:T(8,128)(2,1)S(1)} %copy-done, f32[64,128,128]{2,1,0:T(8,128)} %gather_fusion.2, f32[64,128]{1,0:T(8,128)S(1)} %bitcast.59, pred[64]{0:T(512)(128)(4,1)S(1)} %compare_and_fusion), kind=kOutput, calls=%fused_computation.16 | convolution fusion | flops 1612709888 | bytes 10518592 | tf_op jit(solution)/shard_map/rbj,bij->rbi/dot_general | solution.py:75
  253.3 6.5 %fusion.6 = f32[128,64,128]{2,1,0:T(8,128)S(1)} fusion(f32[128,64,128]{2,0,1:T(8,128)S(1)} %multiply_bitcast_fusion), kind=kOutput, calls=%fused_computation.10 | convolution fusion | flops 1611022336 | bytes 8388608 | tf_op jit(solution)/shard_map/rac,dc->rad/dot_general | solution.py:24
  259.8 3.9 convolution_bitcast_fusion
  263.7 2.8 copy.29
  266.5 60.0 %all_to_all.31 = f32[128,64,128]{2,0,1:T(8,128)S(1)} all-to-all(f32[128,64,128]{2,0,1:T(8,128)S(1)} %copy.29), channel_id=1, replica_groups=mesh['feat'=64,'rows'=2] {'feat'}, dimensions={1} | all-to-all | bytes 8388608 | tf_op jit(solution)/shard_map/all_to_all | solution.py:32
  326.5 6.0 %fusion.16 = f32[128,64,128]{2,1,0:T(8,128)S(1)} fusion(f32[128,64,128]{2,0,1:T(8,128)S(1)} %all_to_all.31), kind=kOutput, calls=%fused_computation.20 | convolution fusion | flops 805396480 | bytes 8388608 | tf_op jit(solution)/shard_map/gwf,aw->gaf/dot_general | solution.py:33
  332.5 4.4 copy.31
  336.9 6.1 %all-to-all-start.5 = ((f32[128,64,128]{2,0,1:T(8,128)}), f32[128,64,128]{2,0,1:T(8,128)}, u32[]{:S(2)}, u32[]{:S(2)}) async-start(f32[128,64,128]{2,0,1:T(8,128)} %copy.31), calls=%async_computation.5 | async-start | bytes 8388608 | tf_op jit(solution)/shard_map/all_to_all | solution.py:39
  343.0 0.6 dynamic-slice
  344.3 0.0 copy-start.5
  344.3 49.6 %all-to-all-done.5 = f32[128,64,128]{2,0,1:T(8,128)} async-done(((f32[128,64,128]{2,0,1:T(8,128)}), f32[128,64,128]{2,0,1:T(8,128)}, u32[]{:S(2)}, u32[]{:S(2)}) %all-to-all-start.5) | async-done | bytes 4194336 | tf_op jit(solution)/shard_map/all_to_all | solution.py:39
  393.9 5.6 %copy.32 = f32[128,64,128]{0,2,1:T(8,128)} copy(f32[128,64,128]{2,0,1:T(8,128)} %all-to-all-done.5) | data formatting | bytes 8388608 | tf_op jit(solution)/shard_map/all_to_all | solution.py:39
  399.5 16.6 %fusion.1 = f32[128,8192]{0,1:T(8,128)S(1)} fusion(f32[128,64,128]{0,2,1:T(8,128)} %copy.32, f32[8192]{0:T(1024)S(1)} %copy-done.5, f32[8192]{0:T(1024)S(1)} %broadcast_multiply_fusion.2), kind=kLoop, calls=%fused_computation.5 | loop fusion | flops 2097152 | bytes 8454144 | tf_op jit(solution)/shard_map/cos | solution.py:83
  416.1 0.0 copy-start.8
  416.1 0.0 copy-start.1
  416.2 2.1 copy-done.2
  418.3 2.3 convolution_bitcast_fusion.2
  420.6 80.4 %all-gather.1 = f32[64,1,128]{2,1,0:T(1,128)S(1)} all-gather(f32[1,1,128]{2,1,0:T(1,128)S(1)} %convolution_bitcast_fusion.2), channel_id=2, replica_groups=mesh['feat'=64,'rows'=2] {'feat'}, dimensions={0}, use_global_device_ids=true | all-gather | bytes 33280 | tf_op jit(solution)/shard_map/all_gather | solution.py:85
  501.0 0.1 reduce_sum.9
  501.1 0.0 copy-start.9
  501.1 5.6 %fusion.36 = f32[1,8192]{1,0:T(1,128)S(1)} fusion(f32[128,8192]{0,1:T(8,128)} %copy-done.2, f32[128]{0:T(128)S(1)} %broadcast_multiply_fusion.3, f32[128]{0:T(128)S(1)} %copy-done.8), kind=kOutput, calls=%fused_computation.58 | convolution fusion | flops 12583040 | bytes 4228096 | tf_op jit(solution)/shard_map/dot_general | solution.py:90
  506.8 11.9 %all-reduce = f32[8192]{0:T(1024)S(1)} all-reduce(f32[8192]{0:T(1024)S(1)} %broadcast_multiply_fusion.1), channel_id=3, replica_groups=mesh['feat'=64,'rows'=2] {'rows'}, use_global_device_ids=true, to_apply=%region_3.5.clone | all-reduce | flops 8192 | bytes 65536
  518.7 0.6 dynamic-slice.1
  (33 shorter events, 0.1 us)
Async XLA Ops:
  0.6 246.1 %copy-start = (bf16[64,128,128]{2,1,0:T(8,128)(2,1)S(1)}, bf16[64,128,128]{2,1,0:T(8,128)(2,1)}, u32[]{:S(2)}) copy-start(bf16[64,128,128]{2,1,0:T(8,128)(2,1)} %param.17) | copy-start | bytes 6291460
  4.2 4.8 copy-start.3
  23.7 9.8 %copy-start.10 = (s32[64]{0:T(128)S(1)}, s32[64]{0:T(128)}, u32[]{:S(2)}) copy-start(s32[64]{0:T(128)} %param.16) | copy-start | bytes 772
  23.7 60.9 %all-to-all-start = ((f32[128,64,128]{2,0,1:T(8,128)}), f32[128,64,128]{2,0,1:T(8,128)}, u32[]{:S(2)}, u32[]{:S(2)}) async-start(f32[128,64,128]{2,0,1:T(8,128)} %copy.25), calls=%async_computation | async-start | bytes 8388608 | tf_op jit(solution)/shard_map/all_to_all | solution.py:32
  84.6 22.1 %all-to-all-start.2 = ((s32[64,1,1]{2,1,0:T(1,128)}), s32[64,1,1]{2,1,0:T(1,128)S(1)}, u32[]{:S(2)}, u32[]{:S(2)}) async-start(s32[64,1,1]{2,1,0:T(1,128)} %copy.24), calls=%async_computation.2 | async-start | bytes 65536 | tf_op jit(solution)/shard_map/all_to_all | solution.py:70
  106.7 60.3 %all-to-all-start.1 = ((f32[128,64,128]{2,0,1:T(8,128)}), f32[128,64,128]{2,0,1:T(8,128)}, u32[]{:S(2)}, u32[]{:S(2)}) async-start(f32[128,64,128]{2,0,1:T(8,128)} %copy.27), calls=%async_computation.1 | async-start | bytes 8388608 | tf_op jit(solution)/shard_map/all_to_all | solution.py:39
  181.3 60.5 %all-to-all-start.3 = ((f32[128,64,128]{2,0,1:T(8,128)}), f32[128,64,128]{2,0,1:T(8,128)}, u32[]{:S(2)}, u32[]{:S(2)}) async-start(f32[128,64,128]{2,0,1:T(8,128)} %select_bitcast_fusion), calls=%async_computation.3 | async-start | bytes 8388608 | tf_op jit(solution)/shard_map/all_to_all | solution.py:73
  192.8 54.0 %copy-start.4 = (f32[8192]{0:T(1024)S(1)}, f32[8192]{0:T(1024)}, u32[]{:S(2)}) copy-start(f32[8192]{0:T(1024)} %param.13) | copy-start | bytes 98308
  336.9 6.1 %copy-start.11 = (u32[128]{0:T(128)S(1)}, u32[128]{0:T(128)}, u32[]{:S(2)}) copy-start(u32[128]{0:T(128)} %constant.78) | copy-start | bytes 1540
  336.9 7.4 %copy-start.7 = (f32[8192]{0:T(1024)S(1)}, f32[8192]{0:T(1024)}, u32[]{:S(2)}) copy-start(f32[8192]{0:T(1024)} %param.14) | copy-start | bytes 98308
  336.9 57.0 %all-to-all-start.5 = ((f32[128,64,128]{2,0,1:T(8,128)}), f32[128,64,128]{2,0,1:T(8,128)}, u32[]{:S(2)}, u32[]{:S(2)}) async-start(f32[128,64,128]{2,0,1:T(8,128)} %copy.31), calls=%async_computation.5 | async-start | bytes 8388608 | tf_op jit(solution)/shard_map/all_to_all | solution.py:39
  344.3 55.2 %copy-start.5 = (f32[8192]{0:T(1024)S(1)}, f32[8192]{0:T(1024)}, u32[]{:S(2)}) copy-start(f32[8192]{0:T(1024)} %param.15) | copy-start | bytes 98308
  399.5 18.8 %copy-start.6 = (f32[8192]{0:T(1024)S(1)}, f32[8192]{0:T(1024)}, u32[]{:S(2)}) copy-start(f32[8192]{0:T(1024)} %param.18) | copy-start | bytes 98308
  416.1 2.1 copy-start.2
  416.1 85.0 %copy-start.8 = (f32[128]{0:T(128)S(1)}, f32[128]{0:T(128)}, u32[]{:S(2)}) copy-start(f32[128]{0:T(128)} %param.19) | copy-start | bytes 1540
  416.1 103.2 %copy-start.1 = (bf16[64,128,128]{2,1,0:T(8,128)(2,1)S(1)}, bf16[64,128,128]{2,1,0:T(8,128)(2,1)}, u32[]{:S(2)}) copy-start(bf16[64,128,128]{2,1,0:T(8,128)(2,1)} %param.17) | copy-start | bytes 6291460
  501.1 18.2 %copy-start.9 = (f32[128]{0:T(128)}, f32[128]{0:T(128)S(1)}, u32[]{:S(2)}) copy-start(f32[128]{0:T(128)S(1)} %broadcast_multiply_fusion.3) | copy-start | bytes 1540
